TPU v7x, 32 devices: a whole 2x2x4 slice. The times are simulated.
32 devices in a mesh: wshard: 4 (over y, x), ctx: 2 (over core), tp: 4 (over z).
Axes of the slice: x: 2, y: 2, z: 4, core: 2. Of those that a mesh axis runs over, the one named last changes fastest.
Arguments:
- tokens: bfloat16 [4, 2048, 768], P('wshard', 'ctx'), may hold values from -6 to 6
- lengths: int32 [4], P('wshard'), may hold values from 512 to 2048, as said below
- qkv_weight: bfloat16 [768, 3, 768], P('wshard', None, 'tp'), may hold values from -0.21875 to 0.21875
- qv_bias: float32 [2, 768], P(None, 'tp'), may hold values from -3 to 3
- out_weight: bfloat16 [768, 768], P('wshard', 'tp'), may hold values from -0.75 to 0.75
- out_bias: float32 [768], replicated, may hold values from -3 to 3
- ln1_gain: float32 [768], replicated, may hold values from 0.5 to 1.5
- ln1_bias: float32 [768], replicated, may hold values from -3 to 3
- gated_weight: bfloat16 [768, 2, 3072], P('wshard', None, 'tp'), may hold values from -0.21875 to 0.21875
- down_weight: bfloat16 [768, 3072], P('wshard', 'tp'), may hold values from -0.109375 to 0.109375
- down_bias: float32 [768], replicated, may hold values from -3 to 3
- ln2_gain: float32 [768], replicated, may hold values from 0.5 to 1.5
- ln2_bias: float32 [768], replicated, may hold values from -3 to 3
- cotangent: bfloat16 [4, 2048, 768], P('wshard', 'ctx'), may hold values from -6 to 6
Outputs:
- layer_output: bfloat16 [4, 2048, 768], P('wshard', 'ctx')
- input_grad: float32 [4, 2048, 768], P('wshard', 'ctx')
- qkv_grad: float32 [768, 3, 768], P('wshard', None, 'tp')
- qvbias_grad: float32 [2, 768], P(None, 'tp')
- outw_grad: float32 [768, 768], P('wshard', 'tp')
- outb_grad: float32 [768], replicated
- ln1g_grad: float32 [768], replicated
- ln1b_grad: float32 [768], replicated
- gated_grad: float32 [768, 2, 3072], P('wshard', None, 'tp')
- down_grad: float32 [768, 3072], P('wshard', 'tp')
- downb_grad: float32 [768], replicated
- ln2g_grad: float32 [768], replicated
- ln2b_grad: float32 [768], replicated
Inputs may be any that keep to these rules, and one draw needn't show every extreme that they name: Each sequence holds lengths[s] valid positions at its start; in every draw some sequence is full (2048) and some has exactly 512.
All inputs are finite; a program needn't handle non-finite values.
Results may differ from a plain program's by a relative error of at most 0.014.
The roundings to bfloat16 on the way count: a program that leaves them out, or rounds other values in their place, can miss the bound.
Values may be sent and summed in bfloat16 or wider, within the bound.
No kernel may reach another device: no remote copies, remote signals or barrier semaphores. Data moves between devices by JAX's collectives and lax.ppermute only.
A program may use at most 128 MiB of HBM per device.

v0:
```python
import jax
import jax.numpy as jnp
from jax import lax
from jax.sharding import PartitionSpec as P

HEADS = 12
DH = 64
norm_eps = 1e-05


def layer_norm(inputs, norm_gain, norm_shift):
    center = inputs - jnp.mean(inputs, axis=-1, keepdims=True)
    spread = jnp.mean(center * center, axis=-1, keepdims=True)
    return center * lax.rsqrt(spread + norm_eps) * norm_gain + norm_shift


def gated_unit(gate_part, up_part):
    return jax.nn.gelu(gate_part, approximate=False) * up_part


def times_transposed(left, right):
    return lax.dot_general(
        left, right, (((1,), (1,)), ((), ())), preferred_element_type=jnp.float32
    )


def first_transposed(left, right):
    return lax.dot_general(
        left, right, (((0,), (0,)), ((), ())), preferred_element_type=jnp.float32
    )


def alibi_scores(queries, key_block, length, query_start, slopes):
    raw_scores = jnp.einsum(
        "qhe,khe->hqk", queries, key_block, preferred_element_type=jnp.float32
    ) * DH ** (-0.5)
    query_pos = query_start + jnp.arange(queries.shape[0], dtype=jnp.int32)
    key_pos = jnp.arange(key_block.shape[0], dtype=jnp.int32)
    distance = jnp.abs(query_pos[:, None] - key_pos[None, :]).astype(jnp.float32)
    biased = raw_scores - slopes[:, None, None] * distance[None, :, :]
    return jnp.where((key_pos < length)[None, None, :], biased, -1e30)


def local(
    tokens,
    lengths,
    qkv_weight,
    qv_bias,
    out_weight,
    out_bias,
    ln1_gain,
    ln1_bias,
    gated_weight,
    down_weight,
    down_bias,
    ln2_gain,
    ln2_bias,
    cotangent,
):
    seq_dev, local_len, model_width = tokens.shape
    row_count = seq_dev * local_len
    part_width = qv_bias.shape[1]
    heads_local = part_width // DH
    ff_local = gated_weight.shape[2]
    shard_rows = qkv_weight.shape[0]
    tp_place = lax.axis_index("tp")
    query_start = lax.axis_index("ctx") * local_len
    head_number = tp_place * heads_local + jnp.arange(heads_local, dtype=jnp.int32) + 1
    slopes = 2.0 ** (-8.0 * head_number.astype(jnp.float32) / HEADS)
    full_qkv, full_out, full_gated, full_down = (
        lax.all_gather(qkv_weight, "wshard", axis=0, tiled=True),
        lax.all_gather(out_weight, "wshard", axis=0, tiled=True),
        lax.all_gather(gated_weight, "wshard", axis=0, tiled=True),
        lax.all_gather(down_weight, "wshard", axis=0, tiled=True),
    )
    token_rows = tokens.reshape(row_count, model_width)
    grad_rows = cotangent.reshape(row_count, model_width)
    projected = jnp.dot(
        token_rows,
        full_qkv.reshape(model_width, 3 * part_width),
        preferred_element_type=jnp.float32,
    ).reshape(row_count, 3, part_width)
    queries = (projected[:, 0] + qv_bias[0]).astype(jnp.bfloat16)
    keys_own = projected[:, 1].astype(jnp.bfloat16)
    values_own = (projected[:, 2] + qv_bias[1]).astype(jnp.bfloat16)
    keys_all, values_all = (
        lax.all_gather(keys_own.reshape(seq_dev, local_len, part_width), "ctx", axis=1, tiled=True),
        lax.all_gather(
            values_own.reshape(seq_dev, local_len, part_width), "ctx", axis=1, tiled=True
        ),
    )
    query_heads = queries.reshape(seq_dev, local_len, heads_local, DH)
    key_heads = keys_all.reshape(seq_dev, -1, heads_local, DH)
    value_heads = values_all.reshape(seq_dev, -1, heads_local, DH)

    def attend(entry):
        query_part, key_part, value_part, length = entry
        scores = alibi_scores(query_part, key_part, length, query_start, slopes)
        row_top = jnp.max(scores, axis=-1, keepdims=True)
        exponent = jnp.exp(scores - row_top)
        row_total = jnp.sum(exponent, axis=-1, keepdims=True)
        weights_low = (exponent / row_total).astype(jnp.bfloat16)
        mixture = jnp.einsum(
            "hqk,khe->qhe", weights_low, value_part, preferred_element_type=jnp.float32
        )
        return (mixture.astype(jnp.bfloat16), (row_top + jnp.log(row_total))[:, :, 0])

    mixture, log_total = lax.map(attend, (query_heads, key_heads, value_heads, lengths))
    mixed_rows = mixture.reshape(row_count, part_width)
    attn_part = times_transposed(mixed_rows, full_out)
    own_grads = grad_rows.astype(jnp.float32)
    pre_first = token_rows.astype(jnp.float32) + (lax.psum(attn_part, "tp") + out_bias)
    norm_first = layer_norm(pre_first, ln1_gain, ln1_bias)
    norm_low = norm_first.astype(jnp.bfloat16)
    gate_up = jnp.dot(
        norm_low, full_gated.reshape(model_width, 2 * ff_local), preferred_element_type=jnp.float32
    ).reshape(row_count, 2, ff_local)
    activation = gated_unit(gate_up[:, 0], gate_up[:, 1]).astype(jnp.bfloat16)
    down_part = times_transposed(activation, full_down)
    pre_second = norm_first + (lax.psum(down_part, "tp") + down_bias)
    layer_rows = layer_norm(pre_second, ln2_gain, ln2_bias)
    unused_second, pull_second = jax.vjp(layer_norm, pre_second, ln2_gain, ln2_bias)
    grad_pre2, gain_two, shift_two = pull_second(own_grads)
    output_low = layer_rows.astype(jnp.bfloat16)
    grad_down = grad_pre2.astype(jnp.bfloat16)
    grad_act = jnp.dot(grad_down, full_down, preferred_element_type=jnp.float32)
    unused_unit, pull_unit = jax.vjp(gated_unit, gate_up[:, 0], gate_up[:, 1])
    grad_gate, grad_up = pull_unit(grad_act)
    grad_gated = (
        jnp.stack([grad_gate, grad_up], axis=1)
        .astype(jnp.bfloat16)
        .reshape(row_count, 2 * ff_local)
    )
    back_part = times_transposed(grad_gated, full_gated.reshape(model_width, 2 * ff_local))
    grad_norm1 = grad_pre2 + lax.psum(back_part, "tp")
    unused_first, pull_first = jax.vjp(layer_norm, pre_first, ln1_gain, ln1_bias)
    grad_pre1, gain_one, shift_one = pull_first(grad_norm1)
    grad_attn = grad_pre1.astype(jnp.bfloat16)
    grad_mixed = jnp.dot(grad_attn, full_out, preferred_element_type=jnp.float32).astype(
        jnp.bfloat16
    )
    grad_heads = grad_mixed.reshape(seq_dev, local_len, heads_local, DH)

    def attend_back(entry):
        query_part, key_part, value_part, length, log_part, grad_part = entry
        scores = alibi_scores(query_part, key_part, length, query_start, slopes)
        attention = jnp.exp(scores - log_part[:, :, None])
        grad_weights = jnp.einsum(
            "qhe,khe->hqk", grad_part, value_part, preferred_element_type=jnp.float32
        )
        row_dot = jnp.sum(grad_weights * attention, axis=-1, keepdims=True)
        grad_scores = (attention * (grad_weights - row_dot)).astype(jnp.bfloat16)
        grad_query = jnp.einsum(
            "hqk,khe->qhe", grad_scores, key_part, preferred_element_type=jnp.float32
        ) * DH ** (-0.5)
        grad_key = jnp.einsum(
            "hqk,qhe->khe", grad_scores, query_part, preferred_element_type=jnp.float32
        ) * DH ** (-0.5)
        grad_value = jnp.einsum(
            "hqk,qhe->khe",
            attention.astype(jnp.bfloat16),
            grad_part,
            preferred_element_type=jnp.float32,
        )
        return (grad_query.astype(jnp.bfloat16), grad_key, grad_value)

    grad_query, grad_key_all, grad_value_all = lax.map(
        attend_back, (query_heads, key_heads, value_heads, lengths, log_total, grad_heads)
    )
    grad_key, grad_value = (
        lax.psum_scatter(
            grad_key_all.reshape(seq_dev, -1, part_width), "ctx", scatter_dimension=1, tiled=True
        ),
        lax.psum_scatter(
            grad_value_all.reshape(seq_dev, -1, part_width), "ctx", scatter_dimension=1, tiled=True
        ),
    )
    query_low = grad_query.reshape(row_count, part_width)
    value_low = grad_value.reshape(row_count, part_width).astype(jnp.bfloat16)
    grad_proj = jnp.stack(
        [query_low, grad_key.reshape(row_count, part_width).astype(jnp.bfloat16), value_low], axis=1
    ).reshape(row_count, 3 * part_width)
    input_part = times_transposed(grad_proj, full_qkv.reshape(model_width, 3 * part_width))
    input_rows = grad_pre1 + lax.psum(input_part, "tp")
    shard_grads = lax.psum_scatter(
        jnp.concatenate(
            [
                first_transposed(token_rows, grad_proj),
                first_transposed(grad_attn, mixed_rows),
                first_transposed(norm_low, grad_gated),
                first_transposed(grad_down, activation),
            ],
            axis=1,
        ),
        "wshard",
        scatter_dimension=0,
        tiled=True,
    )
    shard_grads = lax.psum(shard_grads, "ctx")
    qkv_end = 3 * part_width
    out_end = qkv_end + part_width
    gated_end = out_end + 2 * ff_local
    qkv_grad = shard_grads[:, :qkv_end].reshape(shard_rows, 3, part_width)
    outw_grad = shard_grads[:, qkv_end:out_end]
    gated_grad = shard_grads[:, out_end:gated_end].reshape(shard_rows, 2, ff_local)
    down_grad = shard_grads[:, gated_end:]
    bias_terms = jnp.stack(
        [
            jnp.sum(query_low.astype(jnp.float32), axis=0),
            jnp.sum(value_low.astype(jnp.float32), axis=0),
        ],
        axis=0,
    )
    qvbias_grad, outb_grad, ln1g_grad, ln1b_grad, downb_grad, ln2g_grad, ln2b_grad = lax.psum(
        (
            bias_terms,
            jnp.sum(grad_pre1, axis=0),
            gain_one,
            shift_one,
            jnp.sum(grad_pre2, axis=0),
            gain_two,
            shift_two,
        ),
        ("wshard", "ctx"),
    )
    layer_output = output_low.reshape(seq_dev, local_len, model_width)
    input_grad = input_rows.reshape(seq_dev, local_len, model_width)
    return (
        layer_output,
        input_grad,
        qkv_grad,
        qvbias_grad,
        outw_grad,
        outb_grad,
        ln1g_grad,
        ln1b_grad,
        gated_grad,
        down_grad,
        downb_grad,
        ln2g_grad,
        ln2b_grad,
    )


def solution(mesh):
    return jax.shard_map(
        local,
        mesh=mesh,
        in_specs=(
            P("wshard", "ctx", None),
            P("wshard"),
            P("wshard", None, "tp"),
            P(None, "tp"),
            P("wshard", "tp"),
            P(),
            P(),
            P(),
            P("wshard", None, "tp"),
            P("wshard", "tp"),
            P(),
            P(),
            P(),
            P("wshard", "ctx", None),
        ),
        out_specs=(
            P("wshard", "ctx", None),
            P("wshard", "ctx", None),
            P("wshard", None, "tp"),
            P(None, "tp"),
            P("wshard", "tp"),
            P(),
            P(),
            P(),
            P("wshard", None, "tp"),
            P("wshard", "tp"),
            P(),
            P(),
            P(),
        ),
        check_vma=False,
    )
```

profile of v0, /device:TPU:0, one launch (start us, length us, event | category | flops | bytes accessed | tf_op | source)
XLA Modules:
  0.0 759.2 jit_solution(12784075745873838943)
XLA Ops:
  8.1 17.1 %all_gather.18 = bf16[768,3,192]{2,0,1:T(8,128)(2,1)S(1)} all-gather(bf16[192,3,192]{2,0,1:T(8,128)(2,1)} %param.16), channel_id=1, replica_groups=mesh['wshard'=4,'ctx'=2,'tp'=4] {'wshard'}, dimensions={0}, use_global_device_ids=true | all-gather | bytes 1105920 | tf_op jit(solution)/shard_map/all_gather | solution.py:71
  25.2 1.3 copy.33
  26.6 2.3 fusion.37
  29.0 1.3 copy-done.19
  30.2 2.4 all-gather
  32.7 4.7 abs_convert_fusion
  38.1 1.2 fusion.48
  39.3 2.4 all_gather.19
  41.7 8.5 %all_gather.21 = bf16[768,192]{1,0:T(8,128)(2,1)S(1)} all-gather(bf16[192,192]{1,0:T(8,128)(2,1)S(1)} %copy-done.34), channel_id=1, replica_groups=mesh['wshard'=4,'ctx'=2,'tp'=4] {'wshard'}, dimensions={0}, use_global_device_ids=true | all-gather | bytes 368640 | tf_op jit(solution)/shard_map/all_gather | solution.py:72
  50.2 13.7 %fusion.62 = (f32[3,1024]{1,0:T(4,128)S(1)}, f32[3,1024,2048]{2,1,0:T(8,128)}) fusion(f32[1024,2048]{1,0:T(8,128)} %abs_convert_fusion, f32[3]{0:T(128)S(1)} %multiply_power_fusion, bf16[2048,3,64]{0,2,1:T(8,128)(2,1)S(1)} %bitcast.198, f32[1024,3,64]{0,2,1:T(8,128)S(1)} %bitcast.196, f32[3,64]{1,0:T(4,128)S(1)} %add.174, ...), kind=kOutput, calls=%fused_computation.121 | convolution fusion | flops 837153792 | bytes 35142412 | tf_op jit(solution)/shard_map/while/body/eval_jaxpr/qhe,khe->hqk/dot_general | solution.py:34
  63.9 10.4 %fusion = f32[3,1024]{1,0:T(4,128)S(1)} fusion(f32[3,1024,2048]{2,1,0:T(8,128)} %get-tuple-element.136, f32[3,1024]{1,0:T(4,128)S(1)} %get-tuple-element.135), kind=kLoop, calls=%fused_computation.6 | loop fusion | flops 12579840 | bytes 25190400 | tf_op jit(solution)/shard_map/while/body/eval_jaxpr/reduce_sum | solution.py:101
  74.4 10.6 %fusion.45 = bf16[3,64,1024]{2,1,0:T(8,128)(2,1)S(1)} fusion(bf16[2048,3,64]{0,2,1:T(8,128)(2,1)S(1)} %bitcast.206, f32[3,1024,2048]{2,1,0:T(8,128)} %get-tuple-element.136, f32[3,1024]{1,0:T(4,128)S(1)} %fusion, f32[3,1024]{1,0:T(4,128)S(1)} %get-tuple-element.135), kind=kOutput, calls=%fused_computation.85 | convolution fusion | flops 824377344 | bytes 26370048 | tf_op jit(solution)/shard_map/while/body/eval_jaxpr/hqk,khe->qhe/dot_general | solution.py:103
  85.0 0.7 copy-done.27
  85.7 2.3 fusion.63
  88.1 0.9 copy.34
  89.1 0.5 all-gather.6.cloned.1.call-update
  90.1 119.5 %all-reduce.7.cloned.1.call-done = f32[1024,768]{1,0:T(8,128)} async-done(((f32[1024,768]{1,0:T(8,128)}), f32[1024,768]{1,0:T(8,128)}) %all-reduce.7.cloned.1.call-update) | async-done | bytes 3145744 | tf_op jit(solution)/shard_map/psum | solution.py:112
  209.6 2.8 fusion.61
  213.0 4.3 copy.35
  217.3 4.6 fusion.33
  221.9 2.7 copy-done.11
  224.6 7.8 %multiply_convert_fusion.1 = (bf16[1024,768]{0,1:T(8,128)(2,1)}, f32[1024,768]{0,1:T(8,128)}) fusion(f32[1024,2,768]{0,2,1:T(8,128)S(1)} %fusion.33), kind=kLoop, calls=%fused_computation.46 | loop fusion | flops 51904512 | bytes 11010048 | tf_op jit(solution)/shard_map/convert_element_type | solution.py:118
  232.5 4.9 fusion.64
  237.6 120.0 %all-reduce.9.cloned.1.call-done = f32[1024,768]{1,0:T(8,128)} async-done(((f32[1024,768]{1,0:T(8,128)}), f32[1024,768]{1,0:T(8,128)}) %all-reduce.9.cloned.1.call-update) | async-done | bytes 3145744 | tf_op jit(solution)/shard_map/psum | solution.py:120
  357.6 2.9 fusion.59
  361.1 0.8 copy-done.6
  361.9 1.8 fusion.11
  363.7 2.6 fusion.58
  367.1 3.3 fusion.19
  370.5 1.1 copy-done.24
  372.1 4.4 convolution_bitcast_fusion.1
  376.8 119.9 %all-reduce.11.cloned.1.call-done = f32[1024,768]{1,0:T(8,128)} async-done(((f32[1024,768]{1,0:T(8,128)}), f32[1024,768]{1,0:T(8,128)}) %all-reduce.11.cloned.1.call-update) | async-done | bytes 3145744 | tf_op jit(solution)/shard_map/psum | solution.py:135
  496.8 4.4 multiply_reduce_fusion.1
  501.2 1.5 fusion.57
  502.7 1.6 copy-done.1
  504.3 0.8 convolution_convert_fusion
  505.1 16.4 %multiply_reduce_fusion = (f32[3,1024]{1,0:T(4,128)}, f32[3,1024,2048]{2,1,0:T(8,128)}) fusion(f32[3,1024,2048]{2,1,0:T(8,128)} %get-tuple-element.136, f32[3,1024]{1,0:T(4,128)S(1)} %log_add_fusion, bf16[1024,3,64]{0,2,1:T(8,128)(2,1)S(1)} %bitcast.203, bf16[2048,3,64]{0,2,1:T(8,128)(2,1)} %bitcast.207), kind=kOutput, calls=%fused_computation.1 | convolution fusion | flops 824177664 | bytes 51535872 | tf_op jit(solution)/shard_map/while/body/eval_jaxpr/qhe,khe->hqk/dot_general | solution.py:148
  521.5 17.0 %multiply_convert_fusion = bf16[3,1024,2048]{2,1,0:T(8,128)(2,1)S(1)} fusion(f32[3,1024,2048]{2,1,0:T(8,128)} %get-tuple-element.138, f32[3,1024,2048]{2,1,0:T(8,128)} %get-tuple-element.136, f32[3,1024]{1,0:T(4,128)} %get-tuple-element.137, f32[3,1024]{1,0:T(4,128)S(1)} %log_add_fusion), kind=kLoop, calls=%fused_computation | loop fusion | flops 25165824 | bytes 62939136 | tf_op jit(solution)/shard_map/while/body/eval_jaxpr/convert_element_type | solution.py:152
  538.6 4.0 convolution_multiply_fusion
  542.6 0.9 copy-done
  543.7 12.2 %fusion.2 = f32[3,64,2048]{2,1,0:T(8,128)} fusion(bf16[1024,3,64]{0,2,1:T(8,128)(2,1)S(1)} %bitcast.204, f32[3,1024,2048]{2,1,0:T(8,128)} %get-tuple-element.136, f32[3,1024]{1,0:T(4,128)S(1)} %log_add_fusion), kind=kOutput, calls=%fused_computation.8 | convolution fusion | flops 817889280 | bytes 27144192 | tf_op jit(solution)/shard_map/while/body/eval_jaxpr/hqk,qhe->khe/dot_general | solution.py:159
  556.2 2.3 maximum_convert_fusion
  559.6 3.1 fusion.51
  562.7 5.1 fusion.54
  567.8 0.8 fusion.53
  569.1 4.0 convert_reduce_fusion.2
  573.2 1.3 convert_bitcast_fusion.1
  574.5 1.3 convert_reduce_fusion.1
  575.9 0.6 copy-done.20
  576.5 2.3 fusion.41
  578.8 1.9 copy.37
  580.7 9.9 %concatenate.3 = f32[768,3072]{1,0:T(8,128)} concatenate(f32[768,576]{1,0:T(8,128)S(1)} %copy.37, f32[768,192]{1,0:T(8,128)S(1)} %fusion.53, f32[768,1536]{1,0:T(8,128)} %fusion.54, f32[768,768]{1,0:T(8,128)} %fusion.51), dimensions={1} | concatenate | bytes 18874368 | tf_op jit(solution)/shard_map/concatenate | solution.py:186
  590.7 1.2 copy-done.13
  592.0 3.1 convolution_bitcast_fusion
  595.2 89.0 %reduce-scatter.8.cloned.1.call-done = f32[192,3072]{1,0:T(8,128)} async-done(((f32[768,3072]{1,0:T(8,128)}), f32[192,3072]{1,0:T(8,128)}) %reduce-scatter.8.cloned.1.call-update) | async-done | bytes 2359312 | tf_op jit(solution)/shard_map/reduce_scatter | solution.py:185
  684.3 1.7 convert_reduce_fusion
  686.1 28.9 %all-reduce.13.cloned.1.call-done = f32[1024,768]{1,0:T(8,128)} async-done(((f32[1024,768]{1,0:T(8,128)}), f32[1024,768]{1,0:T(8,128)}) %all-reduce.13.cloned.1.call-update) | async-done | bytes 3145744 | tf_op jit(solution)/shard_map/psum | solution.py:184
  715.0 4.0 add_reduce_fusion
  719.0 24.4 %all-reduce = (f32[2,192]{1,0:T(2,128)}, f32[768]{0:T(1024)}, f32[768]{0:T(1024)}, f32[768]{0:T(1024)}, f32[768]{0:T(1024)}, /*index=5*/f32[768]{0:T(1024)}, f32[768]{0:T(1024)}) all-reduce(f32[2,192]{1,0:T(2,128)S(1)} %pad_maximum_fusion.1, ...), channel_id=1, replica_groups=mesh['wshard'=4,'ctx'=2,'tp'=4] {'wshard','ctx'}, use_global_device_ids=true, to_apply=%region_21.22 | all-reduce | flops 4992 | bytes 39936 | tf_op jit(solution)/shard_map/psum | solution.py:214
  743.4 1.3 slice-done.5
  744.7 1.8 reshape.302
  746.7 1.1 copy.41
  747.7 1.9 slice.55
  749.7 1.8 slice.53
  (162 shorter events, 6.5 us)
Async XLA Ops:
  8.0 18.5 %copy-start.22 = (bf16[1,1024,768]{2,1,0:T(8,128)(2,1)S(1)}, bf16[1,1024,768]{2,1,0:T(8,128)(2,1)}, u32[]{:S(2)}) copy-start(bf16[1,1024,768]{2,1,0:T(8,128)(2,1)} %param.14) | copy-start | bytes 4718596
  8.0 201.6 %all-reduce.7.cloned.1.call-start = ((), (), s32[]{:S(2)}) async-start(), calls=%async_computation.3 | async-start | bytes 6291456 | tf_op jit(solution)/shard_map/psum | solution.py:112
  25.2 3.6 copy-start.12
  28.8 1.4 copy-start.19
  28.9 3.8 copy-start.53
  30.2 19.9 %copy-start.4 = (f32[1024,1,192]{0,2,1:T(8,128)}, f32[1024,1,192]{0,2,1:T(8,128)S(1)}, u32[]{:S(2)}) copy-start(f32[1024,1,192]{0,2,1:T(8,128)S(1)} %slice.48) | copy-start | bytes 2359300
  32.6 17.6 %copy-start.9 = (bf16[2048,1,192]{0,2,1:T(8,128)(2,1)}, bf16[2048,1,192]{0,2,1:T(8,128)(2,1)S(1)}, u32[]{:S(2)}) copy-start(bf16[2048,1,192]{0,2,1:T(8,128)(2,1)S(1)} %all-gather) | copy-start | bytes 2359300
  32.7 17.5 %copy-start.32 = (f32[3,64]{1,0:T(4,128)}, f32[3,64]{1,0:T(4,128)S(1)}, u32[]{:S(2)}) copy-start(f32[3,64]{1,0:T(4,128)S(1)} %add.174) | copy-start | bytes 2308
  32.7 9.0 %copy-start.34 = (bf16[192,192]{1,0:T(8,128)(2,1)S(1)}, bf16[192,192]{1,0:T(8,128)(2,1)}, u32[]{:S(2)}) copy-start(bf16[192,192]{1,0:T(8,128)(2,1)} %param.18) | copy-start | bytes 221188
  41.7 32.7 %copy-start.17 = (bf16[1,2048,192]{1,2,0:T(8,128)(2,1)}, bf16[1,2048,192]{1,2,0:T(8,128)(2,1)S(1)}, u32[]{:S(2)}) copy-start(bf16[1,2048,192]{1,2,0:T(8,128)(2,1)S(1)} %all_gather.19) | copy-start | bytes 2359300
  50.2 34.8 %copy-start.14 = (bf16[768,192]{1,0:T(8,128)(2,1)}, bf16[768,192]{1,0:T(8,128)(2,1)S(1)}, u32[]{:S(2)}) copy-start(bf16[768,192]{1,0:T(8,128)(2,1)S(1)} %all_gather.21) | copy-start | bytes 884740
  85.7 2.4 copy-start.29
  88.0 121.6 %copy-start.48 = (f32[768]{0:T(1024)S(1)}, f32[768]{0:T(1024)}, u32[]{:S(2)}) copy-start(f32[768]{0:T(1024)} %param.19) | copy-start | bytes 9220
  88.1 124.9 %all-gather.4.cloned.1.call-start = ((), (), s32[]{:S(2)}) async-start(), calls=%async_computation.4 | async-start | bytes 2949120 | tf_op jit(solution)/shard_map/all_gather | solution.py:73
  89.0 143.4 %all-gather.6.cloned.1.call-start = ((), (), s32[]{:S(2)}) async-start(), calls=%async_computation.5 | async-start | bytes 1474560 | tf_op jit(solution)/shard_map/all_gather | solution.py:74
  89.6 268.0 %all-reduce.9.cloned.1.call-start = ((), (), s32[]{:S(2)}) async-start(), calls=%async_computation.6 | async-start | bytes 6291456 | tf_op jit(solution)/shard_map/psum | solution.py:120
  212.4 288.7 %copy-start.30 = (f32[1024]{0:T(1024)}, f32[1024]{0:T(1024)S(1)}, u32[]{:S(2)}) copy-start(f32[1024]{0:T(1024)S(1)} %broadcast_multiply_fusion.1) | copy-start | bytes 12292
  212.9 4.4 copy-start.39
  212.9 4.3 copy-start.51
  213.0 288.2 %copy-start.35 = (f32[1024]{0:T(1024)}, f32[1024]{0:T(1024)S(1)}, u32[]{:S(2)}) copy-start(f32[1024]{0:T(1024)S(1)} %fusion.49) | copy-start | bytes 12292
  221.9 2.7 copy-start.11
  237.4 120.2 %copy-start.49 = (f32[768]{0:T(1024)S(1)}, f32[768]{0:T(1024)}, u32[]{:S(2)}) copy-start(f32[768]{0:T(1024)} %param.24) | copy-start | bytes 9220
  237.4 259.4 %all-reduce.11.cloned.1.call-start = ((), (), s32[]{:S(2)}) async-start(), calls=%async_computation.7 | async-start | bytes 6291456 | tf_op jit(solution)/shard_map/psum | solution.py:135
  360.5 1.4 copy-start.6
  361.0 2.7 copy-start.50
  361.9 4.4 slice-start.3
  363.7 2.6 slice-start.4
  363.7 2.9 copy-start.16
  363.7 3.4 copy-start.54
  366.3 4.2 copy-start.7
  366.3 130.4 %copy-start.41 = (f32[1024]{0:T(1024)}, f32[1024]{0:T(1024)S(1)}, u32[]{:S(2)}) copy-start(f32[1024]{0:T(1024)S(1)} %negate_multiply_fusion.2) | copy-start | bytes 12292
  367.1 5.0 copy-start.18
  370.5 1.6 copy-start.25
  376.5 196.6 %reduce-scatter.4.cloned.1.call-start = ((), (), s32[]{:S(2)}) async-start(), calls=%async_computation.8 | async-start | bytes 2359296 | tf_op jit(solution)/shard_map/reduce_scatter | solution.py:171
  501.1 3.1 copy-start.15
  502.6 1.7 copy-start.1
  502.6 2.5 copy-start.37
  521.5 17.0 %copy-start.5 = (f32[1024,1,192]{0,2,1:T(8,128)S(1)}, f32[1024,1,192]{0,2,1:T(8,128)}, u32[]{:S(2)}) copy-start(f32[1024,1,192]{0,2,1:T(8,128)} %copy-done.4) | copy-start | bytes 2359300
  521.5 17.1 %copy-start.33 = (f32[3,64]{1,0:T(4,128)S(1)}, f32[3,64]{1,0:T(4,128)}, u32[]{:S(2)}) copy-start(f32[3,64]{1,0:T(4,128)} %copy-done.32) | copy-start | bytes 2308
  538.6 5.0 copy-start
  543.6 30.9 %reduce-scatter.6.cloned.1.call-start = ((), (), s32[]{:S(2)}) async-start(), calls=%async_computation.9 | async-start | bytes 2359296 | tf_op jit(solution)/shard_map/reduce_scatter | solution.py:174
  555.9 2.7 copy-start.42
  555.9 128.3 %reduce-scatter.8.cloned.1.call-start = ((), (), s32[]{:S(2)}) async-start(), calls=%async_computation.11 | async-start | bytes 11796480 | tf_op jit(solution)/shard_map/reduce_scatter | solution.py:185
  556.2 2.8 copy-start.8
  556.2 3.3 copy-start.26
  559.5 3.1 copy-start.31
  559.5 3.1 copy-start.36
  559.5 3.1 copy-start.40
  559.5 3.1 copy-start.52
  559.5 9.1 %slice-start = ((s8[12582912]{0:T(1024)(128)(4,1)}), s8[4194304]{0:T(1024)(128)(4,1)S(1)}, s32[]{:S(2)}) async-start(s8[12582912]{0:T(1024)(128)(4,1)} %bitcast.193), calls=%async_computation.13 | async-start | bytes 8388608
  559.5 9.1 %slice-start.1 = ((s8[12582912]{0:T(1024)(128)(4,1)}), s8[4194304]{0:T(1024)(128)(4,1)S(1)}, s32[]{:S(2)}) async-start(s8[12582912]{0:T(1024)(128)(4,1)} %bitcast.193), calls=%async_computation.14 | async-start | bytes 8388608
  562.6 5.1 copy-start.2
  562.6 5.1 copy-start.28
  562.6 5.1 copy-start.38
  562.7 6.0 slice-start.2
  573.1 3.4 copy-start.23
  590.7 124.3 %all-reduce.13.cloned.1.call-start = ((), (), s32[]{:S(2)}) async-start(), calls=%async_computation.10 | async-start | bytes 6291456 | tf_op jit(solution)/shard_map/psum | solution.py:184
  595.1 119.9 %copy-start.3 = (f32[1024,768]{1,0:T(8,128)S(1)}, f32[1024,768]{1,0:T(8,128)}, u32[]{:S(2)}) copy-start(f32[1024,768]{1,0:T(8,128)} %copy-done.1) | copy-start | bytes 9437188
  595.1 148.2 %all-reduce.15.cloned.1.call-start = ((), (), s32[]{:S(2)}) async-start(), calls=%async_computation.12 | async-start | bytes 4718592 | tf_op jit(solution)/shard_map/psum | solution.py:199
  686.0 32.9 %copy-start.43 = (f32[768]{0:T(1024)S(1)}, f32[768]{0:T(1024)}, u32[]{:S(2)}) copy-start(f32[768]{0:T(1024)} %get-tuple-element.102) | copy-start | bytes 9220
  686.0 32.9 %copy-start.44 = (f32[768]{0:T(1024)S(1)}, f32[768]{0:T(1024)}, u32[]{:S(2)}) copy-start(f32[768]{0:T(1024)} %get-tuple-element.106) | copy-start | bytes 9220
  686.1 32.9 %copy-start.45 = (f32[768]{0:T(1024)S(1)}, f32[768]{0:T(1024)}, u32[]{:S(2)}) copy-start(f32[768]{0:T(1024)} %get-tuple-element.128) | copy-start | bytes 9220
  686.1 32.9 %copy-start.47 = (f32[768]{0:T(1024)S(1)}, f32[768]{0:T(1024)}, u32[]{:S(2)}) copy-start(f32[768]{0:T(1024)} %get-tuple-element.104) | copy-start | bytes 9220
  743.4 3.1 slice-start.6
  (8 other events, 9.3 us)
Sparse Core Ops, SparseCore 0:
  88.2 121.3 all-reduce.6
  237.5 120.0 all-reduce.8
  376.7 120.0 all-reduce.10
  595.3 119.6 all-reduce.12
  717.2 20.7 all-reduce.14
Sparse Core Ops, SparseCore 1:
  91.0 37.5 all-gather.3
  130.2 27.4 all-gather.5
  543.7 7.8 reduce-scatter.3
  556.0 8.0 reduce-scatter.5
  590.8 93.4 reduce-scatter.7
where the time goes:
time: 768 us; the launch traced here: 759 us
  waiting for transfers between devices  478 us (62%)
  matrix products  98.1 us (13%)
  other arithmetic  68.9 us (9%)
  blocking collectives  54.8 us (7%)
  local copies, waits for them, and re-layouts  40.6 us (5%)
  between operations  17.3 us (2%)
    psum x1, waiting for transfers between devices, local(): pre_second = norm_first + (lax.psum(down_part, 'tp') + down_bias)  120 us
    psum x1, waiting for transfers between devices, local(): grad_norm1 = grad_pre2 + lax.psum(back_part, 'tp')  120 us
    psum x1, waiting for transfers between devices, local(): lax.psum(attn_part, 'tp') + out_bias  119 us
    reduce_scatter x1, waiting for transfers between devices, local(): lax.psum_scatter(jnp.concatenate([first_transposed(token_rows, grad_proj)...  89 us
    psum x1, waiting for transfers between devices, local(): input_rows = grad_pre1 + lax.psum(input_part, 'tp')  28.9 us
    psum x1, blocking collectives, local(): lax.psum((bias_terms, jnp.sum(grad_pre1, axis=0), gain_one, shift_one, jn...  24.4 us
    all_gather x1, blocking collectives, local(): lax.all_gather(qkv_weight, 'wshard', axis=0, tiled=True)  17.1 us
    convert_element_type x1, other arithmetic, attend_back(): grad_scores = (attention * (grad_weights - row_dot)).astype(jnp.bfloat16)  17 us
  transfers between devices with their start and end apart: 10, of which 5 were waited for; matrix products, arithmetic and copies ran while one was open for 8% of the time, Pallas kernels for 0%

commit v1 on v0

--- a/solution.py
+++ b/solution.py
@@ -109,7 +109,9 @@
     mixed_rows = mixture.reshape(row_count, part_width)
     attn_part = times_transposed(mixed_rows, full_out)
     own_grads = grad_rows.astype(jnp.float32)
-    pre_first = token_rows.astype(jnp.float32) + (lax.psum(attn_part, "tp") + out_bias)
+    pre_first = token_rows.astype(jnp.float32) + (
+        jnp.sum(lax.all_gather(attn_part, "tp"), axis=0) + out_bias
+    )
     norm_first = layer_norm(pre_first, ln1_gain, ln1_bias)
     norm_low = norm_first.astype(jnp.bfloat16)
     gate_up = jnp.dot(

time: 768 us -> 978 us (1.27)
  waiting for transfers between devices: 478 us -> 665 us
  other arithmetic: 68.9 us -> 80.2 us
    all_gather x0 -> x1, waiting for transfers between devices: none -> 213 us  [local(): lax.all_gather(attn_part, 'tp')]
    psum x1 -> x0, waiting for transfers between devices: 119 us -> none  [local(): lax.psum(attn_part, 'tp') + out_bias]
    psum x1, waiting for transfers between devices: 28.9 us -> 122 us  [local(): input_rows = grad_pre1 + lax.psum(input_part, 'tp')]
  transfers between devices with their start and end apart: 10 -> 10, of which waited for: 5 -> 6; matrix products, arithmetic and copies ran while one was open for 8% -> 12% of each run, Pallas kernels for 0% -> 0%
where the time goes in v1:
time: 978 us; the launch traced here: 969 us
  waiting for transfers between devices  665 us (68%)
  matrix products  102 us (10%)
  other arithmetic  80.2 us (8%)
  blocking collectives  60.9 us (6%)
  local copies, waits for them, and re-layouts  43.6 us (4%)
  between operations  15.9 us (2%)
    all_gather x1, waiting for transfers between devices, local(): lax.all_gather(attn_part, 'tp')  213 us
    psum x1, waiting for transfers between devices, local(): input_rows = grad_pre1 + lax.psum(input_part, 'tp')  122 us
    psum x1, waiting for transfers between devices, local(): pre_second = norm_first + (lax.psum(down_part, 'tp') + down_bias)  121 us
    psum x1, waiting for transfers between devices, local(): grad_norm1 = grad_pre2 + lax.psum(back_part, 'tp')  119 us
    reduce_scatter x1, waiting for transfers between devices, local(): lax.psum_scatter(jnp.concatenate([first_transposed(token_rows, grad_proj)...  88.6 us
    psum x1, blocking collectives, local(): lax.psum((bias_terms, jnp.sum(grad_pre1, axis=0), gain_one, shift_one, jn...  24.4 us
    all_gather x1, blocking collectives, local(): lax.all_gather(qkv_weight, 'wshard', axis=0, tiled=True)  21.4 us
  transfers between devices with their start and end apart: 10, of which 6 were waited for; matrix products, arithmetic and copies ran while one was open for 12% of the time, Pallas kernels for 0%

profile of v1, /device:TPU:0, one launch (start us, length us, event | category | flops | bytes accessed | tf_op | source)
XLA Modules:
  0.0 969.2 jit_solution(9248503156232428800)
XLA Ops:
  7.2 2.0 copy.34
  9.4 21.4 %all_gather.24 = bf16[768,3,192]{2,0,1:T(8,128)(2,1)S(1)} all-gather(bf16[192,3,192]{2,0,1:T(8,128)(2,1)} %param.16), channel_id=1, replica_groups=mesh['wshard'=4,'ctx'=2,'tp'=4] {'wshard'}, dimensions={0}, use_global_device_ids=true | all-gather | bytes 1105920 | tf_op jit(solution)/shard_map/all_gather | solution.py:71
  30.8 1.3 copy.33
  32.1 2.3 fusion.45
  34.5 1.3 copy-done.20
  35.8 2.4 all-gather
  38.3 4.7 abs_convert_fusion
  43.6 1.2 fusion.57
  44.8 2.4 all_gather.25
  47.2 10.3 %all_gather.27 = bf16[768,192]{1,0:T(8,128)(2,1)S(1)} all-gather(bf16[192,192]{1,0:T(8,128)(2,1)S(1)} %copy-done.36), channel_id=1, replica_groups=mesh['wshard'=4,'ctx'=2,'tp'=4] {'wshard'}, dimensions={0}, use_global_device_ids=true | all-gather | bytes 368640 | tf_op jit(solution)/shard_map/all_gather | solution.py:72
  57.6 13.6 %fusion.68 = (f32[3,1024]{1,0:T(4,128)S(1)}, f32[3,1024,2048]{2,1,0:T(8,128)}) fusion(f32[1024,2048]{1,0:T(8,128)} %abs_convert_fusion, f32[3]{0:T(128)S(1)} %multiply_power_fusion, bf16[2048,3,64]{0,2,1:T(8,128)(2,1)S(1)} %bitcast.223, f32[1024,3,64]{0,2,1:T(8,128)S(1)} %bitcast.220, f32[3,64]{1,0:T(4,128)S(1)} %add.194, ...), kind=kOutput, calls=%fused_computation.129 | convolution fusion | flops 837153792 | bytes 35142412 | tf_op jit(solution)/shard_map/while/body/eval_jaxpr/qhe,khe->hqk/dot_general | solution.py:34
  71.2 10.4 %fusion = f32[3,1024]{1,0:T(4,128)S(1)} fusion(f32[3,1024,2048]{2,1,0:T(8,128)} %get-tuple-element.136, f32[3,1024]{1,0:T(4,128)S(1)} %get-tuple-element.135), kind=kLoop, calls=%fused_computation.6 | loop fusion | flops 12579840 | bytes 25190400 | tf_op jit(solution)/shard_map/while/body/eval_jaxpr/reduce_sum | solution.py:101
  81.7 10.6 %fusion.54 = bf16[3,64,1024]{2,1,0:T(8,128)(2,1)S(1)} fusion(bf16[2048,3,64]{0,2,1:T(8,128)(2,1)S(1)} %bitcast.231, f32[3,1024,2048]{2,1,0:T(8,128)} %get-tuple-element.136, f32[3,1024]{1,0:T(4,128)S(1)} %fusion, f32[3,1024]{1,0:T(4,128)S(1)} %get-tuple-element.135), kind=kOutput, calls=%fused_computation.94 | convolution fusion | flops 824377344 | bytes 26370048 | tf_op jit(solution)/shard_map/while/body/eval_jaxpr/hqk,khe->qhe/dot_general | solution.py:103
  92.3 2.3 fusion.69
  95.9 4.3 copy.35
  100.2 213.0 %all-gather.10.cloned.1.call-done = f32[4096,768]{1,0:T(8,128)} async-done(((f32[1024,768]{1,0:T(8,128)}), f32[4096,768]{1,0:T(8,128)}) %all-gather.10.cloned.1.call-update) | async-done | bytes 12582928 | tf_op jit(solution)/shard_map/all_gather | solution.py:113
  313.2 7.5 reduce_sum.176
  320.7 3.0 fusion.67
  325.6 0.8 fusion.25
  326.4 0.9 copy-done.19
  327.3 2.8 fusion.38
  330.1 2.7 copy-done.10
  332.8 7.9 multiply_convert_fusion.2
  340.9 4.9 fusion.70
  346.0 121.0 %all-reduce.6.cloned.1.call-done = f32[1024,768]{1,0:T(8,128)} async-done(((f32[1024,768]{1,0:T(8,128)}), f32[1024,768]{1,0:T(8,128)}) %all-reduce.6.cloned.1.call-update) | async-done | bytes 3145744 | tf_op jit(solution)/shard_map/psum | solution.py:122
  467.0 2.9 fusion.65
  470.5 0.8 copy-done.6
  471.3 1.8 fusion.11
  473.1 2.6 fusion.64
  476.6 3.4 fusion.49
  480.0 1.1 copy-done.24
  481.6 4.4 convolution_bitcast_fusion.1
  487.0 119.2 %all-reduce.8.cloned.1.call-done = f32[1024,768]{1,0:T(8,128)} async-done(((f32[1024,768]{1,0:T(8,128)}), f32[1024,768]{1,0:T(8,128)}) %all-reduce.8.cloned.1.call-update) | async-done | bytes 3145744 | tf_op jit(solution)/shard_map/psum | solution.py:137
  606.2 4.9 multiply_reduce_fusion.1
  611.2 1.5 fusion.63
  612.7 1.6 copy-done.1
  614.3 0.8 convolution_convert_fusion
  615.2 19.4 %multiply_reduce_fusion = (f32[3,1024]{1,0:T(4,128)S(1)}, f32[3,1024,2048]{2,1,0:T(8,128)}) fusion(f32[3,1024,2048]{2,1,0:T(8,128)} %get-tuple-element.136, f32[3,1024]{1,0:T(4,128)S(1)} %log_add_fusion, bf16[1024,3,64]{0,2,1:T(8,128)(2,1)S(1)} %bitcast.228, bf16[2048,3,64]{0,2,1:T(8,128)(2,1)S(1)} %bitcast.232), kind=kOutput, calls=%fused_computation.1 | convolution fusion | flops 824177664 | bytes 51535872 | tf_op jit(solution)/shard_map/while/body/eval_jaxpr/qhe,khe->hqk/dot_general | solution.py:150
  634.6 16.8 %multiply_convert_fusion = bf16[3,1024,2048]{2,1,0:T(8,128)(2,1)S(1)} fusion(f32[3,1024,2048]{2,1,0:T(8,128)} %get-tuple-element.138, f32[3,1024,2048]{2,1,0:T(8,128)} %get-tuple-element.136, f32[3,1024]{1,0:T(4,128)S(1)} %get-tuple-element.137, f32[3,1024]{1,0:T(4,128)S(1)} %log_add_fusion), kind=kLoop, calls=%fused_computation | loop fusion | flops 25165824 | bytes 62939136 | tf_op jit(solution)/shard_map/while/body/eval_jaxpr/convert_element_type | solution.py:154
  651.4 4.1 convolution_multiply_fusion
  655.5 0.9 copy-done
  656.5 12.2 %fusion.2 = f32[3,64,2048]{2,1,0:T(8,128)} fusion(bf16[1024,3,64]{0,2,1:T(8,128)(2,1)S(1)} %bitcast.229, f32[3,1024,2048]{2,1,0:T(8,128)} %get-tuple-element.136, f32[3,1024]{1,0:T(4,128)S(1)} %log_add_fusion), kind=kOutput, calls=%fused_computation.8 | convolution fusion | flops 817889280 | bytes 27144192 | tf_op jit(solution)/shard_map/while/body/eval_jaxpr/hqk,qhe->khe/dot_general | solution.py:161
  669.1 2.3 pad_maximum_fusion
  672.1 3.0 fusion.60
  675.2 4.4 fusion.43
  679.6 1.7 fusion.62
  681.8 5.2 convert_reduce_fusion.2
  687.0 1.9 convert_bitcast_fusion.1
  688.9 1.4 convert_reduce_fusion.1
  691.0 1.1 pad_maximum_fusion.1
  692.2 2.3 fusion.50
  694.5 2.8 copy.37
  697.3 10.7 %concatenate.3 = f32[768,3072]{1,0:T(8,128)} concatenate(f32[768,576]{1,0:T(8,128)} %copy.37, f32[768,192]{1,0:T(8,128)} %fusion.62, f32[768,1536]{1,0:T(8,128)} %fusion.43, f32[768,768]{1,0:T(8,128)} %fusion.60), dimensions={1} | concatenate | bytes 18874368 | tf_op jit(solution)/shard_map/concatenate | solution.py:188
  708.1 4.7 convolution_bitcast_fusion
  712.8 88.6 %reduce-scatter.8.cloned.1.call-done = f32[192,3072]{1,0:T(8,128)} async-done(((f32[768,3072]{1,0:T(8,128)}), f32[192,3072]{1,0:T(8,128)}) %reduce-scatter.8.cloned.1.call-update) | async-done | bytes 2359312 | tf_op jit(solution)/shard_map/reduce_scatter | solution.py:187
  801.5 1.7 convert_reduce_fusion
  803.3 122.2 %all-reduce.10.cloned.1.call-done = f32[1024,768]{1,0:T(8,128)} async-done(((f32[1024,768]{1,0:T(8,128)}), f32[1024,768]{1,0:T(8,128)}) %all-reduce.10.cloned.1.call-update) | async-done | bytes 3145744 | tf_op jit(solution)/shard_map/psum | solution.py:186
  925.5 4.0 add_reduce_fusion
  929.5 24.4 %all-reduce = (f32[2,192]{1,0:T(2,128)}, f32[768]{0:T(1024)}, f32[768]{0:T(1024)}, f32[768]{0:T(1024)}, f32[768]{0:T(1024)}, /*index=5*/f32[768]{0:T(1024)}, f32[768]{0:T(1024)}) all-reduce(f32[2,192]{1,0:T(2,128)S(1)} %pad_maximum_fusion.2, ...), channel_id=1, replica_groups=mesh['wshard'=4,'ctx'=2,'tp'=4] {'wshard','ctx'}, use_global_device_ids=true, to_apply=%region_21.22 | all-reduce | flops 4992 | bytes 39936 | tf_op jit(solution)/shard_map/psum | solution.py:216
  953.9 1.3 slice-done.5
  955.2 1.8 reshape.391
  957.2 1.1 copy.41
  958.3 1.9 slice.55
  960.2 1.8 slice.53
  (168 shorter events, 9.7 us)
Async XLA Ops:
  7.2 24.9 %copy-start.11 = (bf16[1,1024,768]{2,1,0:T(8,128)(2,1)S(1)}, bf16[1,1024,768]{2,1,0:T(8,128)(2,1)}, u32[]{:S(2)}) copy-start(bf16[1,1024,768]{2,1,0:T(8,128)(2,1)} %param.14) | copy-start | bytes 4718596
  7.2 88.7 %all-gather.6.cloned.1.call-start = ((), (), s32[]{:S(2)}) async-start(), calls=%async_computation.3 | async-start | bytes 2949120 | tf_op jit(solution)/shard_map/all_gather | solution.py:73
  9.3 303.9 %all-gather.10.cloned.1.call-start = ((), (), s32[]{:S(2)}) async-start(), calls=%async_computation.12 | async-start | bytes 15728640 | tf_op jit(solution)/shard_map/all_gather | solution.py:113
  30.8 3.6 copy-start.14
  34.4 3.8 copy-start.55
  35.8 21.8 %copy-start.4 = (f32[1024,1,192]{0,2,1:T(8,128)}, f32[1024,1,192]{0,2,1:T(8,128)S(1)}, u32[]{:S(2)}) copy-start(f32[1024,1,192]{0,2,1:T(8,128)S(1)} %slice.48) | copy-start | bytes 2359300
  38.1 19.4 %copy-start.9 = (bf16[2048,1,192]{0,2,1:T(8,128)(2,1)}, bf16[2048,1,192]{0,2,1:T(8,128)(2,1)S(1)}, u32[]{:S(2)}) copy-start(bf16[2048,1,192]{0,2,1:T(8,128)(2,1)S(1)} %all-gather) | copy-start | bytes 2359300
  38.2 19.3 %copy-start.34 = (f32[3,64]{1,0:T(4,128)}, f32[3,64]{1,0:T(4,128)S(1)}, u32[]{:S(2)}) copy-start(f32[3,64]{1,0:T(4,128)S(1)} %add.194) | copy-start | bytes 2308
  38.3 9.0 copy-start.36
  47.2 34.4 %copy-start.16 = (bf16[1,2048,192]{1,2,0:T(8,128)(2,1)}, bf16[1,2048,192]{1,2,0:T(8,128)(2,1)S(1)}, u32[]{:S(2)}) copy-start(bf16[1,2048,192]{1,2,0:T(8,128)(2,1)S(1)} %all_gather.25) | copy-start | bytes 2359300
  71.2 10.5 %copy-start.29 = (f32[3,1024]{1,0:T(4,128)}, f32[3,1024]{1,0:T(4,128)S(1)}, u32[]{:S(2)}) copy-start(f32[3,1024]{1,0:T(4,128)S(1)} %get-tuple-element.135) | copy-start | bytes 36868
  81.6 10.6 %copy-start.39 = (f32[3,1024]{1,0:T(4,128)}, f32[3,1024]{1,0:T(4,128)S(1)}, u32[]{:S(2)}) copy-start(f32[3,1024]{1,0:T(4,128)S(1)} %fusion) | copy-start | bytes 36868
  92.3 2.3 copy-start.27
  94.6 246.3 %all-gather.8.cloned.1.call-start = ((), (), s32[]{:S(2)}) async-start(), calls=%async_computation.4 | async-start | bytes 1474560 | tf_op jit(solution)/shard_map/all_gather | solution.py:74
  95.3 371.7 %all-reduce.6.cloned.1.call-start = ((), (), s32[]{:S(2)}) async-start(), calls=%async_computation.5 | async-start | bytes 6291456 | tf_op jit(solution)/shard_map/psum | solution.py:122
  313.2 7.5 copy-start.49
  320.7 4.2 copy-start.12
  323.7 1.9 copy-start.3
  323.7 1.9 copy-start.40
  323.7 1.9 copy-start.50
  323.8 143.2 %copy-start.30 = (f32[1024]{0:T(1024)}, f32[1024]{0:T(1024)S(1)}, u32[]{:S(2)}) copy-start(f32[1024]{0:T(1024)S(1)} %broadcast_multiply_fusion.1) | copy-start | bytes 12292
  325.6 141.4 %copy-start.32 = (f32[1024]{0:T(1024)}, f32[1024]{0:T(1024)S(1)}, u32[]{:S(2)}) copy-start(f32[1024]{0:T(1024)S(1)} %fusion.58) | copy-start | bytes 12292
  327.3 2.8 copy-start.22
  330.1 2.7 copy-start.10
  345.7 121.3 %copy-start.51 = (f32[768]{0:T(1024)S(1)}, f32[768]{0:T(1024)}, u32[]{:S(2)}) copy-start(f32[768]{0:T(1024)} %param.21) | copy-start | bytes 9220
  345.8 260.5 %all-reduce.8.cloned.1.call-start = ((), (), s32[]{:S(2)}) async-start(), calls=%async_computation.6 | async-start | bytes 6291456 | tf_op jit(solution)/shard_map/psum | solution.py:137
  470.5 2.7 copy-start.54
  471.3 4.4 slice-start.3
  473.1 2.6 slice-start.4
  473.1 2.9 copy-start.15
  473.1 3.4 copy-start.56
  475.7 4.2 copy-start.7
  475.7 4.2 copy-start.44
  476.5 5.0 copy-start.18
  486.0 200.9 %reduce-scatter.4.cloned.1.call-start = ((), (), s32[]{:S(2)}) async-start(), calls=%async_computation.7 | async-start | bytes 2359296 | tf_op jit(solution)/shard_map/reduce_scatter | solution.py:173
  606.2 4.9 copy-start.43
  606.2 4.9 copy-start.31
  606.2 4.9 copy-start.33
  606.2 4.9 copy-start.41
  612.7 2.5 copy-start.17
  612.7 2.5 copy-start.37
  634.6 16.8 %copy-start.5 = (f32[1024,1,192]{0,2,1:T(8,128)S(1)}, f32[1024,1,192]{0,2,1:T(8,128)}, u32[]{:S(2)}) copy-start(f32[1024,1,192]{0,2,1:T(8,128)} %copy-done.4) | copy-start | bytes 2359300
  634.6 16.8 %copy-start.35 = (f32[3,64]{1,0:T(4,128)S(1)}, f32[3,64]{1,0:T(4,128)}, u32[]{:S(2)}) copy-start(f32[3,64]{1,0:T(4,128)} %copy-done.34) | copy-start | bytes 2308
  651.4 5.0 copy-start
  656.4 32.5 %reduce-scatter.6.cloned.1.call-start = ((), (), s32[]{:S(2)}) async-start(), calls=%async_computation.8 | async-start | bytes 2359296 | tf_op jit(solution)/shard_map/reduce_scatter | solution.py:176
  668.7 2.8 copy-start.8
  668.8 2.8 copy-start.45
  668.8 132.7 %reduce-scatter.8.cloned.1.call-start = ((), (), s32[]{:S(2)}) async-start(), calls=%async_computation.10 | async-start | bytes 11796480 | tf_op jit(solution)/shard_map/reduce_scatter | solution.py:187
  669.1 3.1 copy-start.26
  672.1 3.1 copy-start.23
  672.1 9.2 slice-start
  672.1 9.2 slice-start.1
  675.2 4.4 copy-start.2
  675.2 4.4 copy-start.28
  675.2 4.4 copy-start.38
  675.2 6.6 slice-start.2
  688.9 3.3 copy-start.13
  708.1 217.5 %all-reduce.10.cloned.1.call-start = ((), (), s32[]{:S(2)}) async-start(), calls=%async_computation.9 | async-start | bytes 6291456 | tf_op jit(solution)/shard_map/psum | solution.py:186
  712.8 241.1 %all-reduce.12.cloned.1.call-start = ((), (), s32[]{:S(2)}) async-start(), calls=%async_computation.11 | async-start | bytes 4718592 | tf_op jit(solution)/shard_map/psum | solution.py:201
  803.3 126.2 %copy-start.46 = (f32[768]{0:T(1024)S(1)}, f32[768]{0:T(1024)}, u32[]{:S(2)}) copy-start(f32[768]{0:T(1024)} %get-tuple-element.102) | copy-start | bytes 9220
  803.3 126.2 %copy-start.47 = (f32[768]{0:T(1024)S(1)}, f32[768]{0:T(1024)}, u32[]{:S(2)}) copy-start(f32[768]{0:T(1024)} %get-tuple-element.106) | copy-start | bytes 9220
  803.3 126.2 %copy-start.48 = (f32[768]{0:T(1024)S(1)}, f32[768]{0:T(1024)}, u32[]{:S(2)}) copy-start(f32[768]{0:T(1024)} %get-tuple-element.128) | copy-start | bytes 9220
  803.3 126.2 %copy-start.53 = (f32[768]{0:T(1024)S(1)}, f32[768]{0:T(1024)}, u32[]{:S(2)}) copy-start(f32[768]{0:T(1024)} %get-tuple-element.104) | copy-start | bytes 9220
  953.9 3.1 slice-start.6
  (10 other events, 13.0 us)
Sparse Core Ops, SparseCore 0:
  10.4 44.1 all-gather.5
  94.7 218.4 all-gather.9
  315.1 25.7 all-gather.7
  345.9 121.0 all-reduce.5
  486.1 120.0 all-reduce.7
  656.5 7.9 reduce-scatter.3
  668.9 8.1 reduce-scatter.5
  708.2 93.2 reduce-scatter.7
  804.4 121.0 all-reduce.9
  927.7 20.7 all-reduce.11
